TPU v7x, 512 devices: a whole 4x8x8 slice. The times are simulated.
512 devices in a mesh: ctx: 32 (over z_hi, y, core), tp: 16 (over x, z_lo).
Axes of the slice: x: 4, y: 8, z: 8 (z_hi: 2, z_lo: 4; z = z_hi * 4 + z_lo), core: 2. Of those that a mesh axis runs over, the one named last changes fastest.
Arguments:
- queries: bfloat16 [12288, 4096], P('ctx', 'tp')
- keys: bfloat16 [12288, 4096], P('ctx', 'tp')
- values: bfloat16 [12288, 4096], P('ctx', 'tp')
- out_gate: bfloat16 [12288, 4096], P('ctx', 'tp'), may hold values from -6 to 6
- in_gate: bfloat16 [12288, 4096], P('ctx', 'tp'), may hold values from -6 to 6
- norm_gain: float32 [4096], P('tp'), may hold values from 0.5 to 1.5
- skip_gain: float32 [4096], P('tp'), may hold values from 0.5 to 1.5
- rates: float32 [4096, 16], P('tp'), may hold values from 8.138021e-06 to 0.03
- residues: float32 [4096, 16], P('tp'), may hold values from -1.5 to 1.5
- block_order: int32 [96], replicated, may hold values from 0 to 95, each once
Outputs:
- attn_out: bfloat16 [12288, 4096], P('ctx', 'tp')
- hyena_out: bfloat16 [12288, 4096], P('ctx', 'tp')
Inputs may be any that keep to these rules, and one draw needn't show every extreme that they name: `block_order`: a permutation of the 96 sequence blocks: every block appears once.
All inputs are finite; a program needn't handle non-finite values.
Results may differ from a plain program's by a relative error of at most 0.015.
Values may be sent and summed in bfloat16 or wider, within the bound.
A program may use at most 64 MiB of HBM per device.

v0:
```python
import math

import jax
import jax.numpy as jnp
from jax import lax
from jax.sharding import PartitionSpec as P

HEAD_DIM = 128
BLK = 128
CHAN = 4096


def row_positions(block_order, global_rows):
    block_ids = global_rows // BLK
    table_ids = jnp.arange(block_order.shape[0], dtype=jnp.int32)
    matches = block_ids[:, None] == table_ids[None, :]
    looked = jnp.sum(jnp.where(matches, block_order[None, :], 0), axis=1)
    return looked * BLK + global_rows % BLK


def modal_tables(decay_rate, residue, length):
    offsets = jnp.arange(length + 1, dtype=jnp.float32)
    decays = jnp.exp(-decay_rate[:, :, None] * offsets[None, None, :])
    weight = residue * jnp.sqrt(-jnp.expm1(-2.0 * decay_rate))
    filter_taps = jnp.sum(weight[:, :, None] * decays[:, :, :length], axis=1)
    lane_ids = jnp.arange(length, dtype=jnp.int32)
    offset_diff = lane_ids[:, None] - lane_ids[None, :]
    toeplitz = jnp.where(
        offset_diff[None, :, :] >= 0, filter_taps[:, jnp.clip(offset_diff, 0, length - 1)], 0.0
    )
    carry_in = weight[:, :, None] * decays[:, :, 1:]
    tail_decay = decays[:, :, :length][:, :, ::-1]
    stride_decay = decays[:, :, length]
    return (toeplitz, carry_in, tail_decay, stride_decay)


def prefix_states(block_ends, stride_decay):

    def combine(earlier, later):
        return (earlier[0] * later[0], earlier[1] * later[0] + later[1])

    powers = jnp.broadcast_to(stride_decay[None, :, :], block_ends.shape)
    inclusive = lax.associative_scan(combine, (powers, block_ends), axis=0)[1]
    return jnp.concatenate([jnp.zeros_like(inclusive[:1]), inclusive[:-1]], axis=0)


def full_convolution(wide, decay_rate, residue, block_order):
    nblocks = block_order.shape[0]
    chans = wide.shape[0]
    toeplitz, carry_in, tail_decay, stride_decay = modal_tables(decay_rate, residue, BLK)
    inverse = (
        jnp.zeros((nblocks,), jnp.int32).at[block_order].set(jnp.arange(nblocks, dtype=jnp.int32))
    )
    blocks = wide.astype(jnp.float32).reshape(chans, nblocks, BLK)[:, inverse]
    highest = lax.Precision.HIGHEST
    inside = jnp.einsum("cij,cbj->cbi", toeplitz, blocks, precision=highest)
    block_ends = jnp.einsum("cmj,cbj->bcm", tail_decay, blocks, precision=highest)
    entering = prefix_states(block_ends, stride_decay)
    carried = jnp.einsum("cmi,bcm->cbi", carry_in, entering, precision=highest)
    return (inside + carried)[:, block_order].reshape(chans, nblocks * BLK)


def per_device(
    queries, keys, values, out_gate, in_gate, norm_gain, skip_gain, rates, residues, block_order
):
    tok_rows, columns = queries.shape
    head_local = columns // HEAD_DIM
    my_index = lax.axis_index("ctx")
    query_pos = row_positions(
        block_order, my_index * tok_rows + jnp.arange(tok_rows, dtype=jnp.int32)
    )
    query_heads = queries.reshape(tok_rows, head_local, HEAD_DIM)
    scaling = HEAD_DIM ** (-0.5)
    initial = (
        jnp.full((head_local, tok_rows), -1e30, jnp.float32),
        jnp.zeros((head_local, tok_rows), jnp.float32),
        jnp.zeros((head_local, tok_rows, HEAD_DIM), jnp.float32),
    )
    key_rows = lax.all_gather(keys, "ctx", axis=0, tiled=True)
    value_rows = lax.all_gather(values, "ctx", axis=0, tiled=True)
    tiles = key_rows.shape[0] // tok_rows
    grouped = math.gcd(tiles, max(1, 1024 // tok_rows))
    width_rows = grouped * tok_rows
    key_blocks = key_rows.reshape(tiles // grouped, width_rows, head_local, HEAD_DIM)
    value_blocks = value_rows.reshape(tiles // grouped, width_rows, head_local, HEAD_DIM)
    block_starts = jnp.arange(tiles // grouped, dtype=jnp.int32) * width_rows

    def advance(state, item):
        run_max, run_total, run_sum = state
        key_tile, value_tile, tile_start = item
        key_pos = row_positions(block_order, tile_start + jnp.arange(width_rows, dtype=jnp.int32))
        scores = (
            jnp.einsum("rhd,khd->hrk", query_heads, key_tile, preferred_element_type=jnp.float32)
            * scaling
        )
        scores = jnp.where(key_pos[None, None, :] <= query_pos[None, :, None], scores, -jnp.inf)
        new_max = jnp.maximum(run_max, jnp.max(scores, axis=2))
        rescale = jnp.exp(run_max - new_max)
        weights = jnp.exp(scores - new_max[:, :, None])
        run_total = run_total * rescale + jnp.sum(weights, axis=2)
        run_sum = run_sum * rescale[:, :, None] + jnp.einsum(
            "hrk,khd->hrd",
            weights.astype(jnp.bfloat16),
            value_tile,
            preferred_element_type=jnp.float32,
        )
        return ((new_max, run_total, run_sum), None)

    result_state, _ = lax.scan(advance, initial, (key_blocks, value_blocks, block_starts))
    run_max, run_total, run_sum = result_state
    attn_out = (
        (run_sum / run_total[:, :, None])
        .transpose(1, 0, 2)
        .reshape(tok_rows, columns)
        .astype(jnp.bfloat16)
    )
    attn_f = attn_out.astype(jnp.float32)
    squares = jnp.sum(attn_f * attn_f, axis=1)
    square_sum = lax.psum(squares, "tp")
    scaled = lax.rsqrt(square_sum / CHAN + 1e-06)
    mixed = (attn_f * scaled[:, None] * norm_gain[None, :] * in_gate.astype(jnp.float32)).astype(
        jnp.bfloat16
    )
    flat = mixed.T
    wide = lax.all_to_all(flat, "ctx", split_axis=0, concat_axis=1, tiled=True)
    chan_part = wide.shape[0]
    part_rates = lax.dynamic_slice_in_dim(rates, my_index * chan_part, chan_part, 0)
    part_residues = lax.dynamic_slice_in_dim(residues, my_index * chan_part, chan_part, 0)
    conv_wide = full_convolution(wide, part_rates, part_residues, block_order).astype(jnp.bfloat16)
    long_conv = lax.all_to_all(conv_wide, "ctx", split_axis=1, concat_axis=0, tiled=True).T
    hyena_out = out_gate.astype(jnp.float32) * (
        long_conv.astype(jnp.float32) + skip_gain[None, :] * mixed.astype(jnp.float32)
    )
    return (attn_out, hyena_out.astype(jnp.bfloat16))


def solution(mesh):
    placed = (
        P("ctx", "tp"),
        P("ctx", "tp"),
        P("ctx", "tp"),
        P("ctx", "tp"),
        P("ctx", "tp"),
        P("tp"),
        P("tp"),
        P("tp", None),
        P("tp", None),
        P(),
    )
    return jax.shard_map(
        per_device,
        mesh=mesh,
        in_specs=placed,
        out_specs=(P("ctx", "tp"), P("ctx", "tp")),
        check_vma=False,
    )
```

profile of v0, /device:TPU:1, one launch (start us, length us, event | category | flops | bytes accessed | tf_op | source)
XLA Modules:
  0.0 515.8 jit_solution(10705832998774465644)
XLA Ops:
  14.7 123.5 %all-gather.3.cloned.1.call-done = bf16[12288,256]{1,0:T(8,128)(2,1)} async-done(((bf16[384,256]{1,0:T(8,128)(2,1)}), bf16[12288,256]{1,0:T(8,128)(2,1)}) %all-gather.3.cloned.1.call-update) | async-done | bytes 6291472 | tf_op jit(solution)/shard_map/all_gather | solution.py:79
  138.3 9.8 %reshape.232 = bf16[16,768,2,128]{3,2,1,0:T(2,128)(2,1)} reshape(bf16[12288,256]{1,0:T(8,128)(2,1)} %all-gather.3.cloned.1.call-done) | data formatting | bytes 12582912 | tf_op jit(solution)/shard_map/reshape | solution.py:84
  148.0 108.4 %all-gather.5.cloned.1.call-done = bf16[12288,256]{1,0:T(8,128)(2,1)} async-done(((bf16[384,256]{1,0:T(8,128)(2,1)}), bf16[12288,256]{1,0:T(8,128)(2,1)}) %all-gather.5.cloned.1.call-update) | async-done | bytes 6291472 | tf_op jit(solution)/shard_map/all_gather | solution.py:80
  256.4 9.7 %reshape.233 = bf16[16,768,2,128]{3,2,1,0:T(2,128)(2,1)} reshape(bf16[12288,256]{1,0:T(8,128)(2,1)} %all-gather.5.cloned.1.call-done) | data formatting | bytes 12582912 | tf_op jit(solution)/shard_map/reshape | solution.py:85
  266.2 99.7 %while.17 = (s32[]{:T(128)}, f32[2,384]{1,0:T(2,128)S(1)}, f32[2,384]{1,0:T(2,128)S(1)}, f32[2,384,128]{2,1,0:T(8,128)S(1)}, s32[16]{0:T(128)S(1)}, /*index=5*/s...) while((s32[]{:T(128)}, f32[2,384]{1,0:T(2,128)S(1)}, ...), condition=%wide.region_5.6_spmd.clone, body=%wide.region_1.5_spmd.clone.sunk | while | flops 309315072 | bytes 11669537 | solution.py:109
  268.4 1.7 constant_dynamic-slice_fusion.5
  274.6 1.7 constant_dynamic-slice_fusion.5
  280.9 1.7 constant_dynamic-slice_fusion.5
  287.1 1.7 constant_dynamic-slice_fusion.5
  293.3 1.7 constant_dynamic-slice_fusion.5
  299.6 1.7 constant_dynamic-slice_fusion.5
  305.8 1.7 constant_dynamic-slice_fusion.5
  312.0 1.7 constant_dynamic-slice_fusion.5
  318.3 1.7 constant_dynamic-slice_fusion.5
  324.5 1.7 constant_dynamic-slice_fusion.5
  330.8 1.7 constant_dynamic-slice_fusion.5
  349.4 1.7 constant_dynamic-slice_fusion.5
  355.7 1.7 constant_dynamic-slice_fusion.5
  366.2 34.5 %psum.7 = f32[384]{0:T(512)S(1)} all-reduce(f32[384]{0:T(512)S(1)} %get-tuple-element.262), channel_id=1, replica_groups=mesh['ctx'=32,'tp'=16] {'tp'}, use_global_device_ids=true, to_apply=%region_7.8 | all-reduce | flops 384 | bytes 3072 | tf_op jit(solution)/shard_map/psum | solution.py:119
  401.6 12.3 %all-to-all-start = ((bf16[32,8,384]{2,1,0:T(8,128)(2,1)}), bf16[32,8,384]{2,1,0:T(8,128)(2,1)S(1)}, u32[]{:S(2)}, u32[]{:S(2)}) async-start(bf16[32,8,384]{2,1,0:T(8,128)(2,1)} %bitcast.4), calls=%async_computation | async-start | bytes 393216 | tf_op jit(solution)/shard_map/all_to_all | solution.py:125
  414.0 54.4 %gather_fusion.1 = f32[16384,8]{1,0:T(8,128)} fusion(f32[8,128]{0,1:T(8,128)S(1)} %get-tuple-element.269, s32[16384]{0:T(1024)S(1)} %fusion.34), kind=kCustom, calls=%fused_computation.1 | custom fusion | bytes 1114112 | tf_op jit(solution)/shard_map/gather | solution.py:29
  468.4 5.1 copy.168
  480.7 12.2 %all-to-all-start.1 = ((bf16[8,32,384]{2,0,1:T(8,128)(2,1)}), bf16[8,32,384]{2,0,1:T(8,128)(2,1)S(1)}, u32[]{:S(2)}, u32[]{:S(2)}) async-start(bf16[8,32,384]{2,0,1:T(8,128)(2,1)} %bitcast.15), calls=%async_computation.1 | async-start | bytes 393216 | tf_op jit(solution)/shard_map/all_to_all | solution.py:130
  493.9 13.1 %all-to-all-done.1 = bf16[8,32,384]{2,0,1:T(8,128)(2,1)S(1)} async-done(((bf16[8,32,384]{2,0,1:T(8,128)(2,1)}), bf16[8,32,384]{2,0,1:T(8,128)(2,1)S(1)}, u32[]{:S(2)}, u32[]{:S(2)}) %all-to-all-start.1) | async-done | bytes 196640 | tf_op jit(solution)/shard_map/all_to_all | solution.py:130
  (274 shorter events, 95.4 us)
Async XLA Ops:
  7.2 131.1 %all-gather.3.cloned.1.call-start = ((), (), s32[]{:S(2)}) async-start(), calls=%async_computation.2 | async-start | bytes 6488064 | tf_op jit(solution)/shard_map/all_gather | solution.py:79
  7.9 248.5 %all-gather.5.cloned.1.call-start = ((), (), s32[]{:S(2)}) async-start(), calls=%async_computation.3 | async-start | bytes 6488064 | tf_op jit(solution)/shard_map/all_gather | solution.py:80
  148.0 118.2 %copy-start.1 = (s32[96]{0:T(128)S(1)}, s32[96]{0:T(128)}, u32[]{:S(2)}) copy-start(s32[96]{0:T(128)} %param.21) | copy-start | bytes 1156
  266.2 134.7 %copy-start.2 = (f32[256]{0:T(256)S(1)}, f32[256]{0:T(256)}, u32[]{:S(2)}) copy-start(f32[256]{0:T(256)} %param.17) | copy-start | bytes 3076
  401.6 72.0 %all-to-all-start = ((bf16[32,8,384]{2,1,0:T(8,128)(2,1)}), bf16[32,8,384]{2,1,0:T(8,128)(2,1)S(1)}, u32[]{:S(2)}, u32[]{:S(2)}) async-start(bf16[32,8,384]{2,1,0:T(8,128)(2,1)} %bitcast.4), calls=%async_computation | async-start | bytes 393216 | tf_op jit(solution)/shard_map/all_to_all | solution.py:125
  477.1 15.8 %copy-start = (bf16[384,256]{1,0:T(8,128)(2,1)S(1)}, bf16[384,256]{1,0:T(8,128)(2,1)}, u32[]{:S(2)}) copy-start(bf16[384,256]{1,0:T(8,128)(2,1)} %param.15) | copy-start | bytes 589828
  477.1 29.9 %copy-start.3 = (f32[256]{0:T(256)S(1)}, f32[256]{0:T(256)}, u32[]{:S(2)}) copy-start(f32[256]{0:T(256)} %param.18) | copy-start | bytes 3076
  480.7 26.3 %all-to-all-start.1 = ((bf16[8,32,384]{2,0,1:T(8,128)(2,1)}), bf16[8,32,384]{2,0,1:T(8,128)(2,1)S(1)}, u32[]{:S(2)}, u32[]{:S(2)}) async-start(bf16[8,32,384]{2,0,1:T(8,128)(2,1)} %bitcast.15), calls=%async_computation.1 | async-start | bytes 393216 | tf_op jit(solution)/shard_map/all_to_all | solution.py:130
Sparse Core Ops, SparseCore 0:
  11.4 126.8 all-gather.2
  141.6 114.7 all-gather.4
where the time goes:
time: 517 us; the launch traced here: 516 us
  waiting for transfers between devices  246 us (48%)
  local copies, waits for them, and re-layouts  125 us (24%)
  other arithmetic  39.9 us (8%)
  blocking collectives  34.5 us (7%)
  matrix products  29.6 us (6%)
  starting transfers between devices  24.6 us (5%)
  between operations  14.6 us (3%)
    all_gather x1, waiting for transfers between devices, per_device(): key_rows = lax.all_gather(keys, 'ctx', axis=0, tiled=True)  124 us
    all_gather x1, waiting for transfers between devices, per_device(): value_rows = lax.all_gather(values, 'ctx', axis=0, tiled=True)  108 us
    gather x2, local copies, waits for them, and re-layouts, modal_tables(): filter_taps[:, jnp.clip(offset_diff, 0, length - 1)]  59.6 us
    dynamic_slice x32, local copies, waits for them, and re-layouts, per_device(): lax.scan(advance, initial, (key_blocks, value_blocks, block_starts))  36 us
    psum x1, blocking collectives, per_device(): square_sum = lax.psum(squares, 'tp')  34.5 us
    dot_general x16, matrix products, advance(): jnp.einsum('hrk,khd->hrd', weights.astype(jnp.bfloat16), value_tile, pref...  16.8 us
    all_to_all x1, waiting for transfers between devices, per_device(): lax.all_to_all(conv_wide, 'ctx', split_axis=1, concat_axis=0, tiled=True)  13.1 us
    all_to_all x1, starting transfers between devices, per_device(): wide = lax.all_to_all(flat, 'ctx', split_axis=0, concat_axis=1, tiled=True)  12.3 us
  transfers between devices with their start and end apart: 4, of which 3 were waited for; matrix products, arithmetic and copies ran while one was open for 15% of the time, Pallas kernels for 0%

commit v1 on v0

v1 whole, which is shorter than its diff:
```python
import functools
import math

import jax
import jax.numpy as jnp
from jax import lax
from jax.experimental import pallas as pl
from jax.experimental.pallas import tpu as pltpu
from jax.sharding import PartitionSpec as P

HD = 128
BLK = 128
MODES = 16
NB = 3
ROWS = NB * BLK
EXP_SCALE = math.log2(math.e) / math.sqrt(HD)
NEG = -1e30
MESH = pl.DeviceIdType.MESH
F32 = jnp.float32
BF16 = jnp.bfloat16


def body(
    nctx, ntp, bo_ref, row_of_ref,
    q_ref, k_ref, v_ref, og_ref, ig_ref, ng_ref, sg_ref, dec_ref, wgt_ref, blkdec_ref,
    aout_ref, hout_ref,
    kv, qt, zsend_kv, zsend_q, acc, mx, qpos,
    oz_send, oz_recv, ss_send, ss_recv, sq, xs, ys, mixed,
    ends, gath, prefix, reply, enter,
    ring_ss, ring_rs, sib_ss, sib_rs, z_ss, z_rs, tp_ss, tp_rs, e_ss, e_rs, r_ss, r_rs,
):
    ny = nctx // 4
    half = nctx // 2
    per = MODES // half if MODES >= half else 1
    ctx = lax.axis_index("ctx")
    tp = lax.axis_index("tp")
    core = lax.rem(ctx, 2)
    y = lax.rem(ctx // 2, ny)
    zh = ctx // half
    step_dir = 1 - 2 * core

    def at(z, yy, c):
        return z * half + lax.rem(yy + 2 * ny, ny) * 2 + c

    nxt = (at(zh, y + step_dir, core), tp)
    sib = (at(zh, y, 1 - core), tp)
    partner = (lax.rem(ctx + half, nctx), tp)

    barrier = pltpu.get_barrier_semaphore()

    @pl.loop(1, nctx)
    def _(i):
        pl.semaphore_signal(barrier, inc=1, device_id=(lax.rem(ctx + i, nctx), tp), device_id_type=MESH)

    @pl.loop(1, ntp)
    def _(i):
        pl.semaphore_signal(barrier, inc=1, device_id=(ctx, lax.rem(tp + i, ntp)), device_id_type=MESH)

    own_cols = pl.ds(pl.multiple_of(zh * HD, HD), HD)
    oth_cols = pl.ds(pl.multiple_of((1 - zh) * HD, HD), HD)

    def put_kv(dst, cols):
        dst[0:ROWS, :] = k_ref[:, cols]
        for b in range(NB):
            blk = v_ref[b * BLK:(b + 1) * BLK, cols].astype(F32)
            dst[ROWS + b * BLK:ROWS + (b + 1) * BLK, :] = blk.T.astype(BF16)

    put_kv(kv.at[0, 0, 0], own_cols)
    put_kv(zsend_kv, oth_cols)
    qt[0] = q_ref[:, own_cols].astype(F32).T.astype(BF16)
    zsend_q[...] = q_ref[:, oth_cols].astype(F32).T.astype(BF16)

    pl.semaphore_wait(barrier, nctx - 1 + ntp - 1)

    def ring_copy(s, zz, part):
        rows = pl.ds(part * ROWS, ROWS)
        return pltpu.make_async_remote_copy(
            kv.at[s, zz, 0, rows], kv.at[s + 1, zz, 0, rows],
            ring_ss.at[s, zz, part], ring_rs.at[s + 1, zz, part],
            device_id=nxt, device_id_type=MESH)

    def ring_arrival(s, zz, part):
        rows = pl.ds(part * ROWS, ROWS)
        return pltpu.make_async_remote_copy(
            kv.at[s - 1, zz, 0, rows], kv.at[s, zz, 0, rows],
            ring_ss.at[s - 1, zz, part], ring_rs.at[s, zz, part],
            device_id=nxt, device_id_type=MESH)

    def sib_copy(s, zz):
        return pltpu.make_async_remote_copy(
            kv.at[s, zz, 0], kv.at[s, zz, 1], sib_ss.at[s, zz], sib_rs.at[s, zz],
            device_id=sib, device_id_type=MESH)

    def z_copy(i):
        src, dst = ((zsend_kv.at[0:ROWS], kv.at[0, 1, 0, 0:ROWS]),
                    (zsend_kv.at[ROWS:2 * ROWS], kv.at[0, 1, 0, ROWS:2 * ROWS]),
                    (zsend_q, qt.at[1]),
                    (ss_send, ss_recv),
                    (oz_send, oz_recv))[i]
        return pltpu.make_async_remote_copy(
            src, dst, z_ss.at[i], z_rs.at[i], device_id=partner, device_id_type=MESH)

    ring_copy(0, 0, 0).start()
    z_copy(0).start()
    ring_copy(0, 0, 1).start()
    z_copy(1).start()
    z_copy(2).start()
    sib_copy(0, 0).start()

    lane = lax.broadcasted_iota(jnp.int32, (1, ROWS), 1)
    for zz in range(2):
        dev = at(jnp.where(zz == 0, zh, 1 - zh), y, core)
        p0 = bo_ref[dev * NB]
        p1 = bo_ref[dev * NB + 1]
        p2 = bo_ref[dev * NB + 2]
        qpos[zz] = jnp.where(lane < BLK, p0, jnp.where(lane < 2 * BLK, p1, p2))
    mx[...] = jnp.full(mx.shape, NEG, F32)
    acc[...] = jnp.zeros(acc.shape, F32)
    ones = jnp.ones((16, ROWS), BF16)

    def unit(s, zk, zq):
        qtv = qt[zq]
        qv = qpos[zq]
        zsrc = zh if zk == 0 else 1 - zh
        srcs = (at(zsrc, y - step_dir * s, core), at(zsrc, y + step_dir * s, 1 - core))
        tiles = []
        m_old = mx[zq]
        m_new = m_old
        for d in range(2):
            st = jnp.dot(kv[s, zk, d, 0:ROWS], qtv, preferred_element_type=F32)
            for b in range(NB):
                tile = st[b * BLK:(b + 1) * BLK]
                if d == 0 and zk == zq:
                    rel = (lax.broadcasted_iota(jnp.int32, (BLK, BLK), 0)
                           - lax.broadcasted_iota(jnp.int32, (BLK, BLK), 1))
                    limit = jnp.where(s == 0, 0, BLK)
                    cut = jnp.where(rel <= limit, tile[:, b * BLK:(b + 1) * BLK], -jnp.inf)
                    parts = [tile[:, j * BLK:(j + 1) * BLK] if j != b else cut for j in range(NB)]
                    tile = jnp.concatenate(parts, axis=1)
                vis = bo_ref[srcs[d] * NB + b] <= qv
                m_new = jnp.maximum(m_new, jnp.where(vis, jnp.max(tile, axis=0, keepdims=True), NEG))
                tiles.append((tile, vis))
        mc = m_new * EXP_SCALE
        total = acc[zq] * jnp.exp2(m_old * EXP_SCALE - mc)
        for d in range(2):
            probs = []
            vts = []
            for b in range(NB):
                tile, vis = tiles[d * NB + b]
                probs.append(jnp.exp2(tile * EXP_SCALE - jnp.where(vis, mc, jnp.inf)).astype(BF16))
                vts.append(kv[s, zk, d, ROWS + b * BLK:ROWS + (b + 1) * BLK])
            vt = jnp.concatenate([jnp.concatenate(vts, axis=1), ones], axis=0)
            total = total + jnp.dot(vt, jnp.concatenate(probs, axis=0), preferred_element_type=F32)
        acc[zq] = total
        mx[zq] = m_new

    def take(s, zz, part):
        @pl.when(s < ny)
        def _():
            ring_arrival(s, zz, part).wait_recv()

            @pl.when(s < ny - 1)
            def _():
                ring_copy(s, zz, part).start()

            if part == 1:
                sib_copy(s, zz).start()

    @pl.loop(0, ny)
    def _(s):
        take(s + 1, 0, 0)
        sib_copy(s, 0).wait_recv()
        unit(s, 0, 0)
        take(s + 1, 0, 1)

    z_copy(0).wait_recv()
    ring_copy(0, 1, 0).start()
    z_copy(1).wait_recv()
    ring_copy(0, 1, 1).start()
    sib_copy(0, 1).start()
    z_copy(2).wait_recv()

    @pl.loop(0, ny)
    def _(s):
        unit(s, 0, 1)
        take(s + 1, 1, 0)
        sib_copy(s, 1).wait_recv()
        unit(s, 1, 1)
        take(s + 1, 1, 1)

        @pl.when(s >= 1)
        def _():
            unit(s - 1, 1, 0)

    def finish(zq):
        whole = acc[zq]
        out = (whole[0:HD] / whole[HD:HD + 1]).astype(BF16).astype(F32)
        return jnp.sum(out * out, axis=0, keepdims=True), out.T.astype(BF16)

    squares, out = finish(1)
    ss_send[...] = squares
    oz_send[...] = out
    z_copy(3).start()
    z_copy(4).start()
    unit(ny - 1, 1, 0)
    squares, out = finish(0)
    aout_ref[:, own_cols] = out
    z_copy(3).wait_recv()
    sq[pl.ds(tp, 1)] = (squares + ss_recv[...])[None]

    def tp_copy(i, frm):
        return pltpu.make_async_remote_copy(
            sq.at[frm], sq.at[frm], tp_ss.at[i], tp_rs.at[frm],
            device_id=(ctx, lax.rem(tp + i, ntp)), device_id_type=MESH)

    @pl.loop(1, ntp)
    def _(i):
        tp_copy(i, tp).start()

    z_copy(4).wait_recv()
    aout_ref[:, oth_cols] = oz_recv[...]

    @pl.loop(1, ntp)
    def _(i):
        tp_copy(i, lax.rem(tp + i, ntp)).wait_recv()

    square_sum = jnp.sum(sq[...], axis=0)
    scaled = lax.rsqrt(square_sum / (ntp * 2 * HD) + 1e-06)
    scaled = jnp.broadcast_to(scaled, (BLK, ROWS)).T
    for b in range(NB):
        rows = slice(b * BLK, (b + 1) * BLK)
        for g in range(2):
            cols = slice(g * HD, (g + 1) * HD)
            val = (aout_ref[rows, cols].astype(F32) * scaled[rows] * ng_ref[:, cols]
                   * ig_ref[rows, cols].astype(F32)).astype(BF16)
            mixed[rows, cols] = val
            xs[pl.ds(2 * b + g, BLK, stride=8), :] = val.astype(F32)
    for r in (2 * NB, 2 * NB + 1):
        xs[pl.ds(r, BLK, stride=8), :] = jnp.zeros((BLK, HD), F32)

    def x_at(t):
        return xs[pl.ds(pl.multiple_of(t * 8, 8), 8), :]

    dec = [dec_ref[m] for m in range(MODES)]
    zeros = tuple(jnp.zeros((8, HD), F32) for _ in range(MODES))

    def end_step(t, state):
        x = x_at(t)
        return tuple(state[m] * dec[m] + x for m in range(MODES))

    state = lax.fori_loop(0, BLK, end_step, zeros, unroll=4)
    for m in range(MODES):
        ends[m] = state[m]

    def mode_chip(m):
        return 2 * (m // per)

    def end_copy(m, frm):
        return pltpu.make_async_remote_copy(
            ends.at[m], gath.at[lax.rem(m, per), frm], e_ss.at[m], e_rs.at[lax.rem(m, per), frm],
            device_id=(mode_chip(m), tp), device_id_type=MESH)

    @pl.loop(0, MODES)
    def _(m):
        @pl.when(mode_chip(m) != ctx)
        def _():
            end_copy(m, ctx).start()

        @pl.when(mode_chip(m) == ctx)
        def _():
            gath[lax.rem(m, per), ctx] = ends[m]

    def inside_step(t, state):
        x = x_at(t)
        state = tuple(state[m] * dec[m] + x for m in range(MODES))
        terms = [state[m] * wgt_ref[m] for m in range(MODES)]
        while len(terms) > 1:
            terms = [a + b for a, b in zip(terms[::2], terms[1::2])]
        ys[pl.ds(pl.multiple_of(t * 8, 8), 8), :] = terms[0]
        return state

    def reply_copy(mm, to, chip):
        return pltpu.make_async_remote_copy(
            reply.at[mm, to], enter.at[chip * per + mm], r_ss.at[mm, to], r_rs.at[chip * per + mm],
            device_id=(to, tp), device_id_type=MESH)

    @pl.when(core == 0)
    def _():
        chip = ctx // 2

        @pl.loop(0, nctx)
        def _(frm):
            @pl.when(frm != ctx)
            def _():
                for mm in range(per):
                    end_copy(chip * per + mm, frm).wait_recv()

        for mm in range(per):
            mode = chip * per + mm
            blkdec = blkdec_ref[mode]

            def block_step(p, carry):
                prefix[pl.ds(2 * p, 1), :] = carry[0]
                prefix[pl.ds(2 * p + 1, 1), :] = carry[1]
                code = row_of_ref[p]
                return tuple(
                    carry[g] * blkdec[g:g + 1] + gath[mm, code // 8, pl.ds(lax.rem(code, 8) + g, 1), :]
                    for g in range(2))

            start = (jnp.zeros((1, HD), F32), jnp.zeros((1, HD), F32))
            lax.fori_loop(0, nctx * NB, block_step, start, unroll=4)

            @pl.loop(0, nctx)
            def _(to):
                for b in range(NB):
                    pos = bo_ref[to * NB + b]
                    for g in range(2):
                        reply[mm, to, 2 * b + g:2 * b + g + 1] = prefix[pl.ds(2 * pos + g, 1), :]
                reply[mm, to, 2 * NB:8] = jnp.zeros((8 - 2 * NB, HD), F32)

                @pl.when(to != ctx)
                def _():
                    reply_copy(mm, to, chip).start()

                @pl.when(to == ctx)
                def _():
                    enter[chip * per + mm] = reply[mm, to]

    lax.fori_loop(0, BLK, inside_step, zeros, unroll=2)

    @pl.loop(0, half)
    def _(chip):
        @pl.when(2 * chip != ctx)
        def _():
            for mm in range(per):
                reply_copy(mm, ctx, chip).wait_recv()

    def carry_step(t, state):
        state = tuple(state[m] * dec[m] for m in range(MODES))
        terms = list(state)
        while len(terms) > 1:
            terms = [a + b for a, b in zip(terms[::2], terms[1::2])]
        rows = pl.ds(pl.multiple_of(t * 8, 8), 8)
        ys[rows, :] = ys[rows, :] + terms[0]
        return state

    lax.fori_loop(0, BLK, carry_step, tuple(enter[m] * wgt_ref[m] for m in range(MODES)), unroll=4)

    for b in range(NB):
        rows = slice(b * BLK, (b + 1) * BLK)
        for g in range(2):
            cols = slice(g * HD, (g + 1) * HD)
            conv = ys[pl.ds(2 * b + g, BLK, stride=8), :].astype(BF16).astype(F32)
            hout_ref[rows, cols] = (og_ref[rows, cols].astype(F32) * (
                conv + sg_ref[:, cols] * mixed[rows, cols].astype(F32))).astype(BF16)

    @pl.loop(0, ny)
    def _(s):
        for zz in range(2):
            sib_copy(s, zz).wait_send()

            @pl.when(s < ny - 1)
            def _():
                for part in range(2):
                    ring_copy(s, zz, part).wait_send()

    for i in range(5):
        z_copy(i).wait_send()

    @pl.loop(1, ntp)
    def _(i):
        tp_copy(i, tp).wait_send()

    @pl.loop(0, MODES)
    def _(m):
        @pl.when(mode_chip(m) != ctx)
        def _():
            end_copy(m, ctx).wait_send()

    @pl.when(core == 0)
    def _():
        @pl.loop(0, nctx)
        def _(to):
            @pl.when(to != ctx)
            def _():
                for mm in range(per):
                    reply_copy(mm, to, ctx // 2).wait_send()


def per_device(nctx, ntp, queries, keys, values, out_gate, in_gate, norm_gain, skip_gain, rates, residues, block_order):
    ny = nctx // 4
    nblk = block_order.shape[0]
    per = max(1, MODES // (nctx // 2))
    stored = jnp.arange(nblk, dtype=jnp.int32)
    codes = (stored // NB) * 8 + (stored % NB) * 2
    row_of = jnp.sum(jnp.where(block_order[None, :] == stored[:, None], codes[None, :], 0), axis=1)

    def spread(table):
        tiles = table.T.reshape(MODES, 1, 2, HD)
        return jnp.broadcast_to(tiles, (MODES, 4, 2, HD)).reshape(MODES, 8, HD)

    dec = spread(jnp.exp(-rates))
    wgt = spread(residues * jnp.sqrt(-jnp.expm1(-2.0 * rates)))
    blkdec = spread(jnp.exp(-BLK * rates))
    vmem = pl.BlockSpec(memory_space=pltpu.VMEM)
    smem = pl.BlockSpec(memory_space=pltpu.SMEM)
    dma = pltpu.SemaphoreType.DMA
    return pl.pallas_call(
        functools.partial(body, nctx, ntp),
        out_shape=(jax.ShapeDtypeStruct((ROWS, 2 * HD), BF16), jax.ShapeDtypeStruct((ROWS, 2 * HD), BF16)),
        in_specs=[smem, smem] + [vmem] * 10,
        out_specs=(vmem, vmem),
        scratch_shapes=[
            pltpu.VMEM((ny, 2, 2, 2 * ROWS, HD), BF16),
            pltpu.VMEM((2, HD, ROWS), BF16),
            pltpu.VMEM((2 * ROWS, HD), BF16),
            pltpu.VMEM((HD, ROWS), BF16),
            pltpu.VMEM((2, HD + 16, ROWS), F32),
            pltpu.VMEM((2, 1, ROWS), F32),
            pltpu.VMEM((2, 1, ROWS), jnp.int32),
            pltpu.VMEM((ROWS, HD), BF16),
            pltpu.VMEM((ROWS, HD), BF16),
            pltpu.VMEM((1, ROWS), F32),
            pltpu.VMEM((1, ROWS), F32),
            pltpu.VMEM((ntp, 1, ROWS), F32),
            pltpu.VMEM((BLK * 8, HD), F32),
            pltpu.VMEM((BLK * 8, HD), F32),
            pltpu.VMEM((ROWS, 2 * HD), BF16),
            pltpu.VMEM((MODES, 8, HD), F32),
            pltpu.VMEM((per, nctx, 8, HD), F32),
            pltpu.VMEM((2 * nblk, HD), F32),
            pltpu.VMEM((per, nctx, 8, HD), F32),
            pltpu.VMEM((MODES, 8, HD), F32),
            dma((ny, 2, 2)), dma((ny, 2, 2)), dma((ny, 2)), dma((ny, 2)), dma((5,)), dma((5,)),
            dma((ntp,)), dma((ntp,)), dma((MODES,)), dma((per, nctx)), dma((per, nctx)), dma((MODES,)),
        ],
        compiler_params=pltpu.CompilerParams(
            collective_id=0, has_side_effects=True, vmem_limit_bytes=48 * 1024 * 1024),
    )(block_order, row_of, queries, keys, values, out_gate, in_gate,
      norm_gain.reshape(1, -1), skip_gain.reshape(1, -1), dec, wgt, blkdec)


def solution(mesh):
    placed = (
        P("ctx", "tp"),
        P("ctx", "tp"),
        P("ctx", "tp"),
        P("ctx", "tp"),
        P("ctx", "tp"),
        P("tp"),
        P("tp"),
        P("tp", None),
        P("tp", None),
        P(),
    )
    return jax.shard_map(
        functools.partial(per_device, mesh.shape["ctx"], mesh.shape["tp"]),
        mesh=mesh,
        in_specs=placed,
        out_specs=(P("ctx", "tp"), P("ctx", "tp")),
        check_vma=False,
    )
```

time: 517 us -> 112 us (0.22)
  waiting for transfers between devices: 246 us -> 0 us
  local copies, waits for them, and re-layouts: 125 us -> 5.66 us
  Pallas kernels: 0 us -> 104 us
  other arithmetic: 39.9 us -> 0.92 us
  blocking collectives: 34.5 us -> 0 us
  matrix products: 29.6 us -> 0 us
  starting transfers between devices: 24.6 us -> 0 us
  between operations: 14.6 us -> 0.74 us
    all_gather x2 -> x0, waiting for transfers between devices: 232 us -> none  [the longest x1 124 us: per_device(): key_rows = lax.all_gather(keys, 'ctx', axis=0, tiled=True)]
    pallas_call x0 -> x1, Pallas kernels: none -> 104 us  [per_device(): pl.pallas_call(functools.partial(body, nctx, ntp), out_shape=(jax.ShapeDt...]
    gather x4 -> x0, local copies, waits for them, and re-layouts: 61.6 us -> none  [the longest x2 59.6 us: modal_tables(): filter_taps[:, jnp.clip(offset_diff, 0, length - 1)]]
    dynamic_slice x33 -> x0, local copies, waits for them, and re-layouts: 36.8 us -> none  [the longest x32 36 us: per_device(): lax.scan(advance, initial, (key_blocks, value_blocks, block_starts))]
    psum x1 -> x0, blocking collectives: 34.5 us -> none  [per_device(): square_sum = lax.psum(squares, 'tp')]
    dot_general x35 -> x0, matrix products: 29.6 us -> none  [the longest x16 16.8 us: advance(): jnp.einsum('hrk,khd->hrd', weights.astype(jnp.bfloat16), value_tile, pref...]
    all_to_all x2 -> x0, starting transfers between devices: 24.5 us -> none  [the longest x1 12.3 us: per_device(): wide = lax.all_to_all(flat, 'ctx', split_axis=0, concat_axis=1, tiled=True)]
    reshape x2 -> x0, local copies, waits for them, and re-layouts: 19.5 us -> none  [the longest x1 9.76 us: per_device(): key_rows.reshape(tiles // grouped, width_rows, head_local, HEAD_DIM)]
  transfers between devices with their start and end apart: 4 -> 0, of which waited for: 3 -> 0; matrix products, arithmetic and copies ran while one was open for 15% -> 0% of each run, Pallas kernels for 0% -> 0%
where the time goes in v1:
time: 112 us; the launch traced here: 111 us
  Pallas kernels  104 us (93%)
  local copies, waits for them, and re-layouts  5.66 us (5%)
    pallas_call x1, Pallas kernels, per_device(): pl.pallas_call(functools.partial(body, nctx, ntp), out_shape=(jax.ShapeDt...  104 us
    unnamed x18, local copies, waits for them, and re-layouts  5.56 us

profile of v1, /device:TPU:1, one launch (start us, length us, event | category | flops | bytes accessed | tf_op | source)
XLA Modules:
  0.0 111.3 jit_solution(16243349994561947343)
XLA Ops:
  0.6 0.0 copy-start.7
  0.7 0.6 copy-done.7
  1.3 0.1 select_reduce_fusion.row_of_ref
  1.4 0.0 copy-start.1
  1.4 0.8 exponential_bitcast_fusion
  2.2 0.0 copy-start
  2.3 0.0 copy-start.6
  2.4 0.0 copy-start.5
  2.4 0.0 copy-done.1
  2.4 0.8 copy-done
  3.2 0.0 copy-done.6
  3.2 0.0 copy-done.5
  3.2 0.0 copy-start.2
  3.2 0.9 copy-done.2
  4.1 0.0 copy-start.3
  4.1 0.9 copy-done.3
  5.0 0.0 copy-start.4
  5.0 0.9 copy-done.4
  6.0 104.0 %shard_map.113 = (bf16[384,256]{1,0:T(8,128)(2,1)S(1)}, bf16[384,256]{1,0:T(8,128)(2,1)S(1)}) custom-call(s32[96]{0:T(128)S(1)} %copy-done.7, s32[96]{0:T(128)S(1)} %select_reduce_fusion.row_of_ref, bf16[384,256]{1,0:T(8,128)(2,1)S(1)} %copy-done, bf16[384,256]{1,0:T(8,128)(2,1)S(1)} %copy-done.1, bf16[384,256]{1,0:T(8,128)(2,1)S(1)} %copy-done.2, ...), custom_call_target="tpu_custom_call" | custom-call | tf_op jit(solution)/shard_map/pallas_call | solution.py:408
  110.0 0.7 copy.14
  110.7 0.7 copy.15
  (7 shorter events, 0.1 us)
Async XLA Ops:
  0.6 0.7 copy-start.7
  1.4 1.0 copy-start.1
  2.2 1.0 copy-start
  2.3 0.8 copy-start.6
  2.4 0.8 copy-start.5
  3.2 0.9 copy-start.2
  4.1 0.9 copy-start.3
  5.0 0.9 copy-start.4

commit v2 on v1

--- a/solution.py
+++ b/solution.py
@@ -21,13 +21,15 @@
 
 
 def body(
-    nctx, ntp, bo_ref, row_of_ref,
-    q_ref, k_ref, v_ref, og_ref, ig_ref, ng_ref, sg_ref, dec_ref, wgt_ref, blkdec_ref,
+    nctx, ntp,
+    bo_in,    q_in, k_in, v_in, og_in, ig_in, ng_in, sg_in, rates_in, residues_in,
     aout_ref, hout_ref,
     kv, qt, zsend_kv, zsend_q, acc, mx, qpos,
     oz_send, oz_recv, ss_send, ss_recv, sq, xs, ys, mixed,
     ends, gath, prefix, reply, enter,
-    ring_ss, ring_rs, sib_ss, sib_rs, z_ss, z_rs, tp_ss, tp_rs, e_ss, e_rs, r_ss, r_rs,
+    q_ref, k_ref, v_ref, og_ref, ig_ref, ng_ref, sg_ref, rates, residues, bo_ref, row_vec, row_of_ref,
+    dec_ref, wgt_ref, blkdec_ref, in_sem, row_sem,
+    plus_ss, plus_rs, minus_ss, minus_rs, sib_ss, sib_rs, z_ss, z_rs, tp_ss, tp_rs, e_ss, e_rs, r_ss, r_rs,
 ):
     ny = nctx // 4
     half = nctx // 2
@@ -37,15 +39,23 @@
     core = lax.rem(ctx, 2)
     y = lax.rem(ctx // 2, ny)
     zh = ctx // half
-    step_dir = 1 - 2 * core
+    hs = ny // 2
 
     def at(z, yy, c):
         return z * half + lax.rem(yy + 2 * ny, ny) * 2 + c
 
-    nxt = (at(zh, y + step_dir, core), tp)
+    after = (at(zh, y + 1, core), tp)
+    before = (at(zh, y - 1, core), tp)
     sib = (at(zh, y, 1 - core), tp)
     partner = (lax.rem(ctx + half, nctx), tp)
 
+    loads = [
+        pltpu.make_async_copy(src, dst, in_sem.at[i])
+        for i, (src, dst) in enumerate((
+            (v_in, v_ref), (k_in, k_ref), (q_in, q_ref), (bo_in, bo_ref), (rates_in, rates),
+            (residues_in, residues), (ng_in, ng_ref), (sg_in, sg_ref), (ig_in, ig_ref), (og_in, og_ref)))]
+    for load in loads:
+        load.start()
     barrier = pltpu.get_barrier_semaphore()
 
     @pl.loop(1, nctx)
@@ -65,6 +75,8 @@
             blk = v_ref[b * BLK:(b + 1) * BLK, cols].astype(F32)
             dst[ROWS + b * BLK:ROWS + (b + 1) * BLK, :] = blk.T.astype(BF16)
 
+    for load in loads[:3]:
+        load.wait()
     put_kv(kv.at[0, 0, 0], own_cols)
     put_kv(zsend_kv, oth_cols)
     qt[0] = q_ref[:, own_cols].astype(F32).T.astype(BF16)
@@ -72,19 +84,25 @@
 
     pl.semaphore_wait(barrier, nctx - 1 + ntp - 1)
 
-    def ring_copy(s, zz, part):
+    def plus_copy(j, zz, part):
         rows = pl.ds(part * ROWS, ROWS)
         return pltpu.make_async_remote_copy(
-            kv.at[s, zz, 0, rows], kv.at[s + 1, zz, 0, rows],
-            ring_ss.at[s, zz, part], ring_rs.at[s + 1, zz, part],
-            device_id=nxt, device_id_type=MESH)
-
-    def ring_arrival(s, zz, part):
+            kv.at[j, zz, 0, rows], kv.at[j + 1, zz, 0, rows],
+            plus_ss.at[j, zz, part], plus_rs.at[j, zz, part],
+            device_id=after, device_id_type=MESH)
+
+    def minus_copy(j, zz, part):
         rows = pl.ds(part * ROWS, ROWS)
         return pltpu.make_async_remote_copy(
-            kv.at[s - 1, zz, 0, rows], kv.at[s, zz, 0, rows],
-            ring_ss.at[s - 1, zz, part], ring_rs.at[s, zz, part],
-            device_id=nxt, device_id_type=MESH)
+            kv.at[lax.rem(ny - j, ny), zz, 0, rows], kv.at[ny - 1 - j, zz, 0, rows],
+            minus_ss.at[j, zz, part], minus_rs.at[j, zz, part],
+            device_id=before, device_id_type=MESH)
+
+    def launch(zz, part):
+        if part == 0 or hs > 1:
+            plus_copy(0, zz, part).start()
+        if part == 1 or hs > 1:
+            minus_copy(0, zz, part).start()
 
     def sib_copy(s, zz):
         return pltpu.make_async_remote_copy(
@@ -100,13 +118,15 @@
         return pltpu.make_async_remote_copy(
             src, dst, z_ss.at[i], z_rs.at[i], device_id=partner, device_id_type=MESH)
 
-    ring_copy(0, 0, 0).start()
+    launch(0, 0)
+    z_copy(2).start()
+    launch(0, 1)
+    sib_copy(0, 0).start()
     z_copy(0).start()
-    ring_copy(0, 0, 1).start()
     z_copy(1).start()
-    z_copy(2).start()
-    sib_copy(0, 0).start()
-
+
+    for load in loads[3:6]:
+        load.wait()
     lane = lax.broadcasted_iota(jnp.int32, (1, ROWS), 1)
     for zz in range(2):
         dev = at(jnp.where(zz == 0, zh, 1 - zh), y, core)
@@ -116,81 +136,124 @@
         qpos[zz] = jnp.where(lane < BLK, p0, jnp.where(lane < 2 * BLK, p1, p2))
     mx[...] = jnp.full(mx.shape, NEG, F32)
     acc[...] = jnp.zeros(acc.shape, F32)
-    ones = jnp.ones((16, ROWS), BF16)
-
-    def unit(s, zk, zq):
-        qtv = qt[zq]
-        qv = qpos[zq]
+    ones = jnp.ones((16, 2 * ROWS), BF16)
+
+    def unit(j, zk, zqs=(0, 1)):
+        qtv = jnp.concatenate([qt[zq] for zq in zqs], axis=1)
+        qv = jnp.concatenate([qpos[zq] for zq in zqs], axis=1)
+        m_old = jnp.concatenate([mx[zq] for zq in zqs], axis=1)
         zsrc = zh if zk == 0 else 1 - zh
-        srcs = (at(zsrc, y - step_dir * s, core), at(zsrc, y + step_dir * s, 1 - core))
+        srcs = (at(zsrc, y - j, core), at(zsrc, y - j, 1 - core))
         tiles = []
-        m_old = mx[zq]
         m_new = m_old
         for d in range(2):
-            st = jnp.dot(kv[s, zk, d, 0:ROWS], qtv, preferred_element_type=F32)
+            st = jnp.dot(kv[j, zk, d, 0:ROWS], qtv, preferred_element_type=F32)
             for b in range(NB):
                 tile = st[b * BLK:(b + 1) * BLK]
-                if d == 0 and zk == zq:
+                if d == 0 and zk in zqs:
                     rel = (lax.broadcasted_iota(jnp.int32, (BLK, BLK), 0)
                            - lax.broadcasted_iota(jnp.int32, (BLK, BLK), 1))
-                    limit = jnp.where(s == 0, 0, BLK)
-                    cut = jnp.where(rel <= limit, tile[:, b * BLK:(b + 1) * BLK], -jnp.inf)
-                    parts = [tile[:, j * BLK:(j + 1) * BLK] if j != b else cut for j in range(NB)]
+                    limit = jnp.where(j == 0, 0, BLK)
+                    spot = zqs.index(zk) * NB + b
+                    parts = [tile[:, i * BLK:(i + 1) * BLK] for i in range(NB * len(zqs))]
+                    parts[spot] = jnp.where(rel <= limit, parts[spot], -jnp.inf)
                     tile = jnp.concatenate(parts, axis=1)
                 vis = bo_ref[srcs[d] * NB + b] <= qv
                 m_new = jnp.maximum(m_new, jnp.where(vis, jnp.max(tile, axis=0, keepdims=True), NEG))
                 tiles.append((tile, vis))
         mc = m_new * EXP_SCALE
-        total = acc[zq] * jnp.exp2(m_old * EXP_SCALE - mc)
-        for d in range(2):
-            probs = []
-            vts = []
-            for b in range(NB):
-                tile, vis = tiles[d * NB + b]
-                probs.append(jnp.exp2(tile * EXP_SCALE - jnp.where(vis, mc, jnp.inf)).astype(BF16))
-                vts.append(kv[s, zk, d, ROWS + b * BLK:ROWS + (b + 1) * BLK])
-            vt = jnp.concatenate([jnp.concatenate(vts, axis=1), ones], axis=0)
-            total = total + jnp.dot(vt, jnp.concatenate(probs, axis=0), preferred_element_type=F32)
-        acc[zq] = total
-        mx[zq] = m_new
-
-    def take(s, zz, part):
-        @pl.when(s < ny)
+        probs = [
+            jnp.exp2(tile * EXP_SCALE - jnp.where(vis, mc, jnp.inf)).astype(BF16) for tile, vis in tiles]
+        vts = [
+            kv[j, zk, d, ROWS + b * BLK:ROWS + (b + 1) * BLK] for d in range(2) for b in range(NB)]
+        vt = jnp.concatenate([jnp.concatenate(vts, axis=1), ones], axis=0)
+        summed = jnp.dot(vt, jnp.concatenate(probs, axis=0), preferred_element_type=F32)
+        scale = jnp.exp2(m_old * EXP_SCALE - mc)
+        for i, zq in enumerate(zqs):
+            cols = slice(i * ROWS, (i + 1) * ROWS)
+            acc[zq] = acc[zq] * scale[:, cols] + summed[:, cols]
+            mx[zq] = m_new[:, cols]
+
+    def take(t, zz, part):
+        far = hs + 1 if part == 0 else hs
+        near = hs + 1 if part == 1 else hs
+
+        @pl.when(t < far)
         def _():
-            ring_arrival(s, zz, part).wait_recv()
-
-            @pl.when(s < ny - 1)
-            def _():
-                ring_copy(s, zz, part).start()
-
-            if part == 1:
-                sib_copy(s, zz).start()
-
-    @pl.loop(0, ny)
-    def _(s):
-        take(s + 1, 0, 0)
-        sib_copy(s, 0).wait_recv()
-        unit(s, 0, 0)
-        take(s + 1, 0, 1)
-
+            plus_copy(t - 1, zz, part).wait_recv()
+
+            @pl.when(t + 1 < far)
+            def _():
+                plus_copy(t, zz, part).start()
+
+        @pl.when(t < near)
+        def _():
+            minus_copy(t - 1, zz, part).wait_recv()
+
+            @pl.when(t + 1 < near)
+            def _():
+                minus_copy(t, zz, part).start()
+
+        if part == 1:
+            sib_copy(t, zz).start()
+
+            @pl.when(t < hs)
+            def _():
+                sib_copy(ny - t, zz).start()
+
+    def walk(zz):
+        @pl.loop(0, hs)
+        def _(s):
+            take(s + 1, zz, 0)
+            sib_copy(s, zz).wait_recv()
+            unit(s, zz)
+            take(s + 1, zz, 1)
+
+            @pl.when(s > 0)
+            def _():
+                sib_copy(ny - s, zz).wait_recv()
+                unit(ny - s, zz)
+
+    nblk = nctx * NB
+    spot = lax.broadcasted_iota(jnp.int32, (1, BLK), 1)
+
+    def place(i, codes):
+        code = lax.div(i, NB) * 8 + lax.rem(i, NB) * 2
+        return jnp.where(spot == bo_ref[i], code, codes)
+
+    row_vec[...] = lax.fori_loop(0, nblk, place, jnp.zeros((1, BLK), jnp.int32), unroll=4)
+    row_copy = pltpu.make_async_copy(row_vec, row_of_ref, row_sem.at[0])
+    row_copy.start()
+    even = lax.rem(lax.broadcasted_iota(jnp.int32, (8, HD), 0), 2) == 0
+
+    @pl.loop(0, MODES)
+    def _(m):
+        def pair(ref):
+            row = ref[pl.ds(m, 1), :]
+            return jnp.where(even, row[:, 0:HD], row[:, HD:2 * HD])
+
+        rate = pair(rates)
+        two = 2.0 * rate
+        series = 1.0 - two * (1 / 6)
+        for k in (5, 4, 3, 2):
+            series = 1.0 - two * series * (1 / k)
+        dec_ref[m] = jnp.exp(-rate)
+        blkdec_ref[m] = jnp.exp(-BLK * rate)
+        wgt_ref[m] = pair(residues) * jnp.sqrt(two * series)
+
+    row_copy.wait()
+    z_copy(2).wait_recv()
+    walk(0)
     z_copy(0).wait_recv()
-    ring_copy(0, 1, 0).start()
+    launch(1, 0)
     z_copy(1).wait_recv()
-    ring_copy(0, 1, 1).start()
+    launch(1, 1)
     sib_copy(0, 1).start()
-    z_copy(2).wait_recv()
-
-    @pl.loop(0, ny)
-    def _(s):
-        unit(s, 0, 1)
-        take(s + 1, 1, 0)
-        sib_copy(s, 1).wait_recv()
-        unit(s, 1, 1)
-        take(s + 1, 1, 1)
-
-        @pl.when(s >= 1)
-        def _():
-            unit(s - 1, 1, 0)
+    sib_copy(hs, 0).wait_recv()
+    unit(hs, 0)
+    walk(1)
+    sib_copy(hs, 1).wait_recv()
+    unit(hs, 1, (1,))
 
     def finish(zq):
         whole = acc[zq]
@@ -202,7 +265,7 @@
     oz_send[...] = out
     z_copy(3).start()
     z_copy(4).start()
-    unit(ny - 1, 1, 0)
+    unit(hs, 1, (0,))
     squares, out = finish(0)
     aout_ref[:, own_cols] = out
     z_copy(3).wait_recv()
@@ -224,6 +287,8 @@
     def _(i):
         tp_copy(i, lax.rem(tp + i, ntp)).wait_recv()
 
+    for load in loads[6:]:
+        load.wait()
     square_sum = jnp.sum(sq[...], axis=0)
     scaled = lax.rsqrt(square_sum / (ntp * 2 * HD) + 1e-06)
     scaled = jnp.broadcast_to(scaled, (BLK, ROWS)).T
@@ -302,7 +367,7 @@
             def block_step(p, carry):
                 prefix[pl.ds(2 * p, 1), :] = carry[0]
                 prefix[pl.ds(2 * p + 1, 1), :] = carry[1]
-                code = row_of_ref[p]
+                code = row_of_ref[0, p]
                 return tuple(
                     carry[g] * blkdec[g:g + 1] + gath[mm, code // 8, pl.ds(lax.rem(code, 8) + g, 1), :]
                     for g in range(2))
@@ -355,14 +420,20 @@
                 conv + sg_ref[:, cols] * mixed[rows, cols].astype(F32))).astype(BF16)
 
     @pl.loop(0, ny)
-    def _(s):
+    def _(j):
         for zz in range(2):
-            sib_copy(s, zz).wait_send()
-
-            @pl.when(s < ny - 1)
-            def _():
-                for part in range(2):
-                    ring_copy(s, zz, part).wait_send()
+            sib_copy(j, zz).wait_send()
+
+    @pl.loop(0, hs)
+    def _(j):
+        for zz in range(2):
+            plus_copy(j, zz, 0).wait_send()
+            minus_copy(j, zz, 1).wait_send()
+
+            @pl.when(j < hs - 1)
+            def _():
+                plus_copy(j, zz, 1).wait_send()
+                minus_copy(j, zz, 0).wait_send()
 
     for i in range(5):
         z_copy(i).wait_send()
@@ -391,24 +462,13 @@
     ny = nctx // 4
     nblk = block_order.shape[0]
     per = max(1, MODES // (nctx // 2))
-    stored = jnp.arange(nblk, dtype=jnp.int32)
-    codes = (stored // NB) * 8 + (stored % NB) * 2
-    row_of = jnp.sum(jnp.where(block_order[None, :] == stored[:, None], codes[None, :], 0), axis=1)
-
-    def spread(table):
-        tiles = table.T.reshape(MODES, 1, 2, HD)
-        return jnp.broadcast_to(tiles, (MODES, 4, 2, HD)).reshape(MODES, 8, HD)
-
-    dec = spread(jnp.exp(-rates))
-    wgt = spread(residues * jnp.sqrt(-jnp.expm1(-2.0 * rates)))
-    blkdec = spread(jnp.exp(-BLK * rates))
     vmem = pl.BlockSpec(memory_space=pltpu.VMEM)
-    smem = pl.BlockSpec(memory_space=pltpu.SMEM)
+    hbm = pl.BlockSpec(memory_space=pltpu.HBM)
     dma = pltpu.SemaphoreType.DMA
     return pl.pallas_call(
         functools.partial(body, nctx, ntp),
         out_shape=(jax.ShapeDtypeStruct((ROWS, 2 * HD), BF16), jax.ShapeDtypeStruct((ROWS, 2 * HD), BF16)),
-        in_specs=[smem, smem] + [vmem] * 10,
+        in_specs=[hbm] * 10,
         out_specs=(vmem, vmem),
         scratch_shapes=[
             pltpu.VMEM((ny, 2, 2, 2 * ROWS, HD), BF16),
@@ -431,13 +491,18 @@
             pltpu.VMEM((2 * nblk, HD), F32),
             pltpu.VMEM((per, nctx, 8, HD), F32),
             pltpu.VMEM((MODES, 8, HD), F32),
-            dma((ny, 2, 2)), dma((ny, 2, 2)), dma((ny, 2)), dma((ny, 2)), dma((5,)), dma((5,)),
+            *[pltpu.VMEM((ROWS, 2 * HD), BF16)] * 5, *[pltpu.VMEM((1, 2 * HD), F32)] * 2,
+            *[pltpu.VMEM((MODES, 2 * HD), F32)] * 2, pltpu.SMEM((nblk,), jnp.int32),
+            pltpu.VMEM((1, BLK), jnp.int32), pltpu.SMEM((1, BLK), jnp.int32),
+            *[pltpu.VMEM((MODES, 8, HD), F32)] * 3, dma((10,)), dma((1,)),
+            dma((ny // 2, 2, 2)), dma((ny // 2, 2, 2)), dma((ny // 2, 2, 2)), dma((ny // 2, 2, 2)),
+            dma((ny, 2)), dma((ny, 2)), dma((5,)), dma((5,)),
             dma((ntp,)), dma((ntp,)), dma((MODES,)), dma((per, nctx)), dma((per, nctx)), dma((MODES,)),
         ],
         compiler_params=pltpu.CompilerParams(
-            collective_id=0, has_side_effects=True, vmem_limit_bytes=48 * 1024 * 1024),
-    )(block_order, row_of, queries, keys, values, out_gate, in_gate,
-      norm_gain.reshape(1, -1), skip_gain.reshape(1, -1), dec, wgt, blkdec)
+            collective_id=0, has_side_effects=True, vmem_limit_bytes=62 * 1024 * 1024),
+    )(block_order, queries, keys, values, out_gate, in_gate,
+      norm_gain.reshape(1, -1), skip_gain.reshape(1, -1), rates.T, residues.T)
 
 
 def solution(mesh):

time: 112 us -> 99.9 us (0.89)
  Pallas kernels: 104 us -> 96.7 us
  local copies, waits for them, and re-layouts: 5.66 us -> 2.34 us
    pallas_call x1, Pallas kernels: 104 us -> 96.7 us  [per_device(): pl.pallas_call(functools.partial(body, nctx, ntp), out_shape=(jax.ShapeDt...]
    unnamed x18 -> x4, local copies, waits for them, and re-layouts: 5.56 us -> 2.34 us
where the time goes in v2:
time: 99.9 us; the launch traced here: 99.7 us
  Pallas kernels  96.7 us (97%)
  local copies, waits for them, and re-layouts  2.34 us (2%)
    pallas_call x1, Pallas kernels, per_device(): pl.pallas_call(functools.partial(body, nctx, ntp), out_shape=(jax.ShapeDt...  96.7 us
    unnamed x4, local copies, waits for them, and re-layouts  2.34 us

profile of v2, /device:TPU:1, one launch (start us, length us, event | category | flops | bytes accessed | tf_op | source)
XLA Modules:
  0.0 99.7 jit_solution(13490481095459536356)
XLA Ops:
  0.6 96.7 %shard_map.113 = (bf16[384,256]{1,0:T(8,128)(2,1)}, bf16[384,256]{1,0:T(8,128)(2,1)}) custom-call(s32[96]{0:T(128)} %bo_in.1, bf16[384,256]{1,0:T(8,128)(2,1)} %q_in.1, bf16[384,256]{1,0:T(8,128)(2,1)} %k_in.1, bf16[384,256]{1,0:T(8,128)(2,1)} %v_in.1, bf16[384,256]{1,0:T(8,128)(2,1)} %og_in.1, bf16[384,256]{1,0:T(8,128)(2,1)} %ig_in.1, f32[1,256]{1,0:T(1,128)} %bitcast.6, ...), custom_call_target="tpu_custom_call" | custom-call | tf_op jit(solution)/shard_map/pallas_call | solution.py:468
  97.4 0.0 copy-start
  97.4 1.7 %copy.14 = bf16[384,256]{1,0:T(8,128)(2,1)} copy(bf16[384,256]{1,0:T(8,128)(2,1)} %get-tuple-element.4) | data formatting | bytes 393216
  99.0 0.0 copy-done
  99.0 0.7 copy.15
Async XLA Ops:
  97.4 1.7 %copy-start = (bf16[384,256]{1,0:T(8,128)(2,1)S(1)}, bf16[384,256]{1,0:T(8,128)(2,1)}, u32[]{:S(2)}) copy-start(bf16[384,256]{1,0:T(8,128)(2,1)} %get-tuple-element.5) | copy-start | bytes 589828

commit v3 on v2

--- a/solution.py
+++ b/solution.py
@@ -201,19 +201,7 @@
             def _():
                 sib_copy(ny - t, zz).start()
 
-    def walk(zz):
-        @pl.loop(0, hs)
-        def _(s):
-            take(s + 1, zz, 0)
-            sib_copy(s, zz).wait_recv()
-            unit(s, zz)
-            take(s + 1, zz, 1)
-
-            @pl.when(s > 0)
-            def _():
-                sib_copy(ny - s, zz).wait_recv()
-                unit(ny - s, zz)
-
+    take(1, 0, 0)
     nblk = nctx * NB
     spot = lax.broadcasted_iota(jnp.int32, (1, BLK), 1)
 
@@ -224,6 +212,7 @@
     row_vec[...] = lax.fori_loop(0, nblk, place, jnp.zeros((1, BLK), jnp.int32), unroll=4)
     row_copy = pltpu.make_async_copy(row_vec, row_of_ref, row_sem.at[0])
     row_copy.start()
+    take(1, 0, 1)
     even = lax.rem(lax.broadcasted_iota(jnp.int32, (8, HD), 0), 2) == 0
 
     @pl.loop(0, MODES)
@@ -243,15 +232,41 @@
 
     row_copy.wait()
     z_copy(2).wait_recv()
-    walk(0)
+
+    def attend(j, zz):
+        sib_copy(j, zz).wait_recv()
+        unit(j, zz)
+
+    @pl.loop(0, hs - 1)
+    def _(s):
+        take(s + 2, 0, 0)
+        attend(s, 0)
+        take(s + 2, 0, 1)
+
+        @pl.when(s > 0)
+        def _():
+            attend(ny - s, 0)
+
     z_copy(0).wait_recv()
     launch(1, 0)
     z_copy(1).wait_recv()
     launch(1, 1)
     sib_copy(0, 1).start()
-    sib_copy(hs, 0).wait_recv()
-    unit(hs, 0)
-    walk(1)
+
+    @pl.loop(hs - 1, min(hs + 2, ny))
+    def _(j):
+        attend(j, 0)
+
+    @pl.loop(0, hs)
+    def _(s):
+        take(s + 1, 1, 0)
+        attend(s, 1)
+        take(s + 1, 1, 1)
+
+        @pl.when(s > 0)
+        def _():
+            attend(ny - s, 1)
+
     sib_copy(hs, 1).wait_recv()
     unit(hs, 1, (1,))
 
@@ -344,6 +359,8 @@
         ys[pl.ds(pl.multiple_of(t * 8, 8), 8), :] = terms[0]
         return state
 
+    lax.fori_loop(0, BLK, inside_step, zeros, unroll=2)
+
     def reply_copy(mm, to, chip):
         return pltpu.make_async_remote_copy(
             reply.at[mm, to], enter.at[chip * per + mm], r_ss.at[mm, to], r_rs.at[chip * per + mm],
@@ -390,8 +407,6 @@
                 @pl.when(to == ctx)
                 def _():
                     enter[chip * per + mm] = reply[mm, to]
-
-    lax.fori_loop(0, BLK, inside_step, zeros, unroll=2)
 
     @pl.loop(0, half)
     def _(chip):

time: 99.9 us -> 94.4 us (0.945)
  Pallas kernels: 96.7 us -> 91.3 us
    pallas_call x1, Pallas kernels: 96.7 us -> 91.3 us  [per_device(): pl.pallas_call(functools.partial(body, nctx, ntp), out_shape=(jax.ShapeDt...]
where the time goes in v3:
time: 94.4 us; the launch traced here: 94.2 us
  Pallas kernels  91.3 us (97%)
  local copies, waits for them, and re-layouts  2.34 us (2%)
    pallas_call x1, Pallas kernels, per_device(): pl.pallas_call(functools.partial(body, nctx, ntp), out_shape=(jax.ShapeDt...  91.3 us
    unnamed x4, local copies, waits for them, and re-layouts  2.34 us

profile of v3, /device:TPU:1, one launch (start us, length us, event | category | flops | bytes accessed | tf_op | source)
XLA Modules:
  0.0 94.2 jit_solution(10337063249729406217)
XLA Ops:
  0.6 91.3 %shard_map.113 = (bf16[384,256]{1,0:T(8,128)(2,1)}, bf16[384,256]{1,0:T(8,128)(2,1)}) custom-call(s32[96]{0:T(128)} %bo_in.1, bf16[384,256]{1,0:T(8,128)(2,1)} %q_in.1, bf16[384,256]{1,0:T(8,128)(2,1)} %k_in.1, bf16[384,256]{1,0:T(8,128)(2,1)} %v_in.1, bf16[384,256]{1,0:T(8,128)(2,1)} %og_in.1, bf16[384,256]{1,0:T(8,128)(2,1)} %ig_in.1, f32[1,256]{1,0:T(1,128)} %bitcast.6, ...), custom_call_target="tpu_custom_call" | custom-call | tf_op jit(solution)/shard_map/pallas_call | solution.py:483
  91.9 0.0 copy-start
  91.9 1.7 %copy.14 = bf16[384,256]{1,0:T(8,128)(2,1)} copy(bf16[384,256]{1,0:T(8,128)(2,1)} %get-tuple-element.4) | data formatting | bytes 393216
  93.6 0.0 copy-done
  93.6 0.7 copy.15
Async XLA Ops:
  91.9 1.7 %copy-start = (bf16[384,256]{1,0:T(8,128)(2,1)S(1)}, bf16[384,256]{1,0:T(8,128)(2,1)}, u32[]{:S(2)}) copy-start(bf16[384,256]{1,0:T(8,128)(2,1)} %get-tuple-element.5) | copy-start | bytes 589828

commit v4 on v3

--- a/solution.py
+++ b/solution.py
@@ -237,35 +237,46 @@
         sib_copy(j, zz).wait_recv()
         unit(j, zz)
 
-    @pl.loop(0, hs - 1)
-    def _(s):
-        take(s + 2, 0, 0)
-        attend(s, 0)
-        take(s + 2, 0, 1)
-
-        @pl.when(s > 0)
-        def _():
-            attend(ny - s, 0)
-
-    z_copy(0).wait_recv()
-    launch(1, 0)
-    z_copy(1).wait_recv()
-    launch(1, 1)
-    sib_copy(0, 1).start()
-
-    @pl.loop(hs - 1, min(hs + 2, ny))
-    def _(j):
-        attend(j, 0)
-
-    @pl.loop(0, hs)
-    def _(s):
-        take(s + 1, 1, 0)
-        attend(s, 1)
-        take(s + 1, 1, 1)
-
-        @pl.when(s > 0)
-        def _():
-            attend(ny - s, 1)
+    def launch_far():
+        z_copy(0).wait_recv()
+        launch(1, 0)
+        z_copy(1).wait_recv()
+        launch(1, 1)
+        sib_copy(0, 1).start()
+
+    def lead(zz, first, last, shift):
+        @pl.loop(first, last)
+        def _(s):
+            take(s + shift, zz, 0)
+            attend(s, zz)
+            take(s + shift, zz, 1)
+
+            @pl.when(s > 0)
+            def _():
+                attend(ny - s, zz)
+
+    def rest(zz, first, last):
+        @pl.loop(first, last)
+        def _(j):
+            attend(j, zz)
+
+    if hs > 2:
+        lead(0, 0, hs - 2, 2)
+        launch_far()
+        rest(0, hs - 2, hs - 1)
+        take(hs, 0, 0)
+        take(hs, 0, 1)
+        rest(0, hs + 2, hs + 3)
+        take(1, 1, 0)
+        take(1, 1, 1)
+        rest(0, hs - 1, hs + 2)
+        rest(1, 0, 1)
+        lead(1, 1, hs, 1)
+    else:
+        lead(0, 0, hs - 1, 2)
+        launch_far()
+        rest(0, hs - 1, min(hs + 2, ny))
+        lead(1, 0, hs, 1)
 
     sib_copy(hs, 1).wait_recv()
     unit(hs, 1, (1,))
@@ -390,7 +401,7 @@
                     for g in range(2))
 
             start = (jnp.zeros((1, HD), F32), jnp.zeros((1, HD), F32))
-            lax.fori_loop(0, nctx * NB, block_step, start, unroll=4)
+            lax.fori_loop(0, nctx * NB, block_step, start, unroll=8)
 
             @pl.loop(0, nctx)
             def _(to):

time: 94.4 us -> 93.6 us (level)
  no operation moved by 1% of the time
where the time goes in v4:
time: 93.6 us; the launch traced here: 93.4 us
  Pallas kernels  90.4 us (97%)
  local copies, waits for them, and re-layouts  2.34 us (2%)
    pallas_call x1, Pallas kernels, per_device(): pl.pallas_call(functools.partial(body, nctx, ntp), out_shape=(jax.ShapeDt...  90.4 us
    unnamed x4, local copies, waits for them, and re-layouts  2.34 us

profile of v4, /device:TPU:1, one launch (start us, length us, event | category | flops | bytes accessed | tf_op | source)
XLA Modules:
  0.0 93.4 jit_solution(14569484653400144438)
XLA Ops:
  0.6 90.4 %shard_map.113 = (bf16[384,256]{1,0:T(8,128)(2,1)}, bf16[384,256]{1,0:T(8,128)(2,1)}) custom-call(s32[96]{0:T(128)} %bo_in.1, bf16[384,256]{1,0:T(8,128)(2,1)} %q_in.1, bf16[384,256]{1,0:T(8,128)(2,1)} %k_in.1, bf16[384,256]{1,0:T(8,128)(2,1)} %v_in.1, bf16[384,256]{1,0:T(8,128)(2,1)} %og_in.1, bf16[384,256]{1,0:T(8,128)(2,1)} %ig_in.1, f32[1,256]{1,0:T(1,128)} %bitcast.6, ...), custom_call_target="tpu_custom_call" | custom-call | tf_op jit(solution)/shard_map/pallas_call | solution.py:494
  91.1 0.0 copy-start
  91.1 1.7 %copy.14 = bf16[384,256]{1,0:T(8,128)(2,1)} copy(bf16[384,256]{1,0:T(8,128)(2,1)} %get-tuple-element.4) | data formatting | bytes 393216
  92.7 0.0 copy-done
  92.8 0.7 copy.15
Async XLA Ops:
  91.1 1.7 %copy-start = (bf16[384,256]{1,0:T(8,128)(2,1)S(1)}, bf16[384,256]{1,0:T(8,128)(2,1)}, u32[]{:S(2)}) copy-start(bf16[384,256]{1,0:T(8,128)(2,1)} %get-tuple-element.5) | copy-start | bytes 589828
